TPU v7x, 128 devices: a whole 4x4x4 slice. The times are simulated.
128 devices in a mesh: dp: 32 (over z, x, core), mp: 4 (over y).
Axes of the slice: x: 4, y: 4, z: 4, core: 2. Of those that a mesh axis runs over, the one named last changes fastest.
Arguments:
- acts: bfloat16 [24576, 4, 1984], P('dp', 'mp'), may hold values from -6 to 6
- grads: bfloat16 [24576, 4, 1984], P('dp', 'mp'), may hold values from -0.21875 to 0.21875
- error: bfloat16 [32, 4, 1984, 1984], P('dp', 'mp'), may hold values from -4 to 4
- momentum: float32 [4, 1984, 1984], P('mp', 'dp'), may hold values from -4 to 4
- q_start: float32 [4, 1984, 128], P('mp'), may hold values from -0.125 to 0.125
Outputs:
- error_next: bfloat16 [32, 4, 1984, 1984], P('dp', 'mp')
- momentum_next: float32 [4, 1984, 1984], P('mp', 'dp')
- q_next: float32 [4, 1984, 128], P('mp')
All inputs are finite; a program needn't handle non-finite values.
Results may differ from a plain program's by a relative error of at most 0.001.
Values sent between devices are 32-bit elements; how exact they have to be, the bound alone decides.
A program may use at most 128 MiB of HBM per device.

v0:
```python
import jax
import jax.numpy as jnp
from jax import lax
from jax.experimental import pallas as pl
from jax.experimental.pallas import tpu as pltpu
from jax.sharding import Mesh
from jax.sharding import PartitionSpec as P

D = 3968
DP = ("dp_0", "dp_1", "dp_2")
MESH = pl.DeviceIdType.MESH
TILE = 1984
PAD = 2048
RANK = 128
TOK = 768
CH = 128
NCH = 16
PIECE = 256
F32 = jnp.float32
BF16 = jnp.bfloat16
PRECISE = lax.Precision.HIGHEST
ORDER = (2, 1, 3, 0)
N_MSG = 27


def mm(a, b):
    return jnp.dot(a, b, preferred_element_type=F32)


def mm_t(a, b):
    return lax.dot_general(a, b, (((1,), (1,)), ((), ())), preferred_element_type=F32)


def split(v):
    hi = v.astype(BF16)
    return hi, (v - hi.astype(F32)).astype(BF16)


class Sum:
    def __init__(self, pos, bufs, sems, base):
        self.z, self.x, self.c, self.y = pos
        self.xs, self.sib, self.buf, self.relay, self.slots, self.out = bufs
        self.send, self.recv = sems
        self.base = base
        self.started = []
        z, x, c = self.z, self.x, self.c
        self.p = (1 - c) * x + c * z
        self.q = (1 - c) * z + c * x
        self.other_p = c * x + (1 - c) * z

    def along_first(self, d):
        return (lax.rem(self.z + self.c * d, 4), lax.rem(self.x + (1 - self.c) * d, 4), self.c, self.y)

    def along_second(self, d):
        return (lax.rem(self.z + (1 - self.c) * d, 4), lax.rem(self.x + self.c * d, 4), self.c, self.y)

    def sibling(self):
        return (self.z, self.x, 1 - self.c, self.y)

    def copy(self, i, src, dst, to):
        made = pltpu.make_async_remote_copy(
            src_ref=src,
            dst_ref=dst,
            send_sem=self.send.at[self.base + i],
            recv_sem=self.recv.at[self.base + i],
            device_id=to,
            device_id_type=MESH,
        )
        made.start()
        self.started.append(made)
        return made

    def sibling_piece(self, n):
        pos = lax.rem(self.other_p + ORDER[n], 4)
        return 4 * (1 - self.c) + pos

    def own_piece(self, n):
        return 4 * self.c + lax.rem(self.p + ORDER[n], 4)

    def send_sibling(self, n):
        i = 2 * self.sibling_piece(n)
        self.from_sibling = getattr(self, "from_sibling", {})
        self.from_sibling[n] = self.copy(n, self.xs.at[pl.ds(i, 2)], self.sib.at[n], self.sibling())

    def own_ready(self, n):
        i = 2 * self.own_piece(n)
        self.from_sibling[n].wait_recv()
        for s in range(2):
            self.xs[i + s] = self.xs[i + s] + self.sib[n, s]
        right, left = self.along_first(1), self.along_first(3)
        if n == 0:
            self.a_r = self.copy(4, self.xs.at[i], self.buf.at[0], right)
            self.a_l = self.copy(5, self.xs.at[i + 1], self.buf.at[1], left)
        elif n == 1:
            self.d_r = self.copy(6, self.xs.at[i + 1], self.buf.at[2], right)
        elif n == 2:
            self.d_l = self.copy(7, self.xs.at[i], self.buf.at[3], left)

    def pass_on(self):
        right, left = self.along_first(1), self.along_first(3)
        self.a_r.wait_recv()
        self.relay[0] = self.xs[2 * self.own_piece(1)] + self.buf[0]
        self.b_r = self.copy(8, self.relay.at[0], self.buf.at[4], right)
        self.a_l.wait_recv()
        self.relay[1] = self.xs[2 * self.own_piece(2) + 1] + self.buf[1]
        self.b_l = self.copy(9, self.relay.at[1], self.buf.at[5], left)

    def finish_first(self):
        i = 2 * self.own_piece(3)
        self.b_r.wait_recv()
        self.d_l.wait_recv()
        self.slots[2 * self.q] = self.xs[i] + self.buf[4] + self.buf[3]
        self.d_r.wait_recv()
        self.b_l.wait_recv()
        self.slots[2 * self.q + 1] = self.xs[i + 1] + self.buf[2] + self.buf[5]

    def spread(self, base, ref, at, right, left):
        own = ref.at[at], ref.at[at + 1]
        r0 = self.copy(base, own[0], own[0], right)
        l1 = self.copy(base + 1, own[1], own[1], left)
        r1 = self.copy(base + 2, own[1], own[1], right)
        l0 = self.copy(base + 3, own[0], own[0], left)
        return r0, l1, r1, l0

    def spread_on(self, base, ref, sent, from_left, from_right, right, left):
        r0, l1, _, _ = sent
        r0.wait_recv()
        f_r = self.copy(base + 4, ref.at[from_left], ref.at[from_left], right)
        l1.wait_recv()
        f_l = self.copy(base + 5, ref.at[from_right + 1], ref.at[from_right + 1], left)
        return f_r, f_l

    def second_start(self):
        self.s_sent = self.spread(10, self.slots, 2 * self.q, self.along_second(1), self.along_second(3))

    def second_pass_on(self):
        lf, rt = 2 * lax.rem(self.q + 3, 4), 2 * lax.rem(self.q + 1, 4)
        self.s_on = self.spread_on(10, self.slots, self.s_sent, lf, rt, self.along_second(1), self.along_second(3))

    def second_finish(self):
        for made in (*self.s_sent[2:], *self.s_on):
            made.wait_recv()
        own = 8 * self.c + 2 * self.p
        for s in range(2):
            self.out[own + s] = (self.slots[s] + self.slots[2 + s]) + (self.slots[4 + s] + self.slots[6 + s])

    def third_start(self):
        own = 8 * self.c + 2 * self.p
        self.t_sent = self.spread(16, self.out, own, self.along_first(1), self.along_first(3))
        part = self.out.at[pl.ds(own, 2)]
        self.to_sib = [self.copy(22, part, part, self.sibling())]

    def third_pass_on(self):
        h = 8 * self.c
        lf, rt = h + 2 * lax.rem(self.p + 3, 4), h + 2 * lax.rem(self.p + 1, 4)
        self.t_on = self.spread_on(16, self.out, self.t_sent, lf, rt, self.along_first(1), self.along_first(3))
        self.t_sent[2].wait_recv()
        part = self.out.at[pl.ds(lf, 2)]
        self.to_sib.append(self.copy(23, part, part, self.sibling()))
        self.t_sent[3].wait_recv()
        part = self.out.at[pl.ds(rt, 2)]
        self.to_sib.append(self.copy(24, part, part, self.sibling()))

    def third_finish(self):
        op = 8 * self.c + 2 * lax.rem(self.p + 2, 4)
        for s in range(2):
            self.t_on[s].wait_recv()
            part = self.out.at[op + s]
            self.to_sib.append(self.copy(25 + s, part, part, self.sibling()))

    def wait_sibling(self):
        for made in self.to_sib:
            made.wait_recv()

    def wait_sends(self):
        for made in self.started:
            made.wait_send()


def body(
    at_hbm, gt_hbm, e_hbm, q_hbm,
    merged_hbm, oo_ref, qq_ref, qn_ref, norm_ref,
    at, gt, e, q, qs, pt, lt, stage, gj, nb, qt,
    xs1, sib1, buf1, relay1, slots1, y1,
    xs2, sib2, buf2, relay2, slots2, y2,
    in_sem, stage_sem, send, recv, n_send, n_recv,
):
    z, x, c, y = (lax.axis_index(a) for a in (*DP, "mp"))
    pos = (z, x, c, y)
    loads = [
        pltpu.make_async_copy(q_hbm, q, in_sem.at[0]),
        pltpu.make_async_copy(gt_hbm, gt.at[pl.ds(0, TILE)], in_sem.at[1]),
        pltpu.make_async_copy(at_hbm, at.at[pl.ds(0, TILE)], in_sem.at[2]),
        pltpu.make_async_copy(e_hbm, e.at[pl.ds(0, TILE)], in_sem.at[3]),
    ]
    for load in loads:
        load.start()
    one = Sum(pos, (xs1, sib1, buf1, relay1, slots1, y1), (send, recv), 0)
    two = Sum(pos, (xs2, sib2, buf2, relay2, slots2, y2), (send, recv), N_MSG)

    barrier = pltpu.get_barrier_semaphore()
    peers = [one.along_first(1), one.along_first(3), one.along_second(1), one.along_second(3), one.sibling()]
    peers += [(z, x, c, lax.rem(y + d, 4)) for d in (1, 2, 3)]
    for peer in peers:
        pl.semaphore_signal(barrier, inc=1, device_id=peer, device_id_type=MESH)

    for ref in (at, gt, e):
        ref[pl.ds(TILE, PAD - TILE), :] = jnp.zeros((PAD - TILE, ref.shape[1]), BF16)

    loads[0].wait()
    hi, lo = split(q[...])
    qs[:, :RANK] = hi
    qs[:, RANK:] = lo
    for i in range(NCH):
        rows = min(CH, TILE - i * CH)
        t_hi, t_lo = split(q[pl.ds(i * CH, rows), :].T)
        lt[:RANK, pl.ds(i * CH, rows)] = t_hi
        lt[RANK:, pl.ds(i * CH, rows)] = t_lo
    lt[:, pl.ds(TILE, PAD - TILE)] = jnp.zeros((2 * RANK, PAD - TILE), BF16)
    loads[1].wait()

    def tokens(ref):
        for n in range(TOK // PIECE):
            cols = pl.ds(n * PIECE, PIECE)
            v = mm(lt[...], ref[:, cols])
            v_hi, v_lo = split(v[:RANK] + v[RANK:])
            pt[:RANK, cols] = v_hi
            pt[RANK:, cols] = v_lo

    tokens(gt)
    loads[2].wait()
    loads[3].wait()

    def left_piece(piece):
        rows = pl.ds(pl.multiple_of(piece * PIECE, PIECE), PIECE)
        v = mm(e[rows, :], qs[...]) + mm_t(at[rows, :], pt[...])
        v = v[:, :RANK] + v[:, RANK:]
        xs1[2 * piece] = v[:CH]
        xs1[2 * piece + 1] = v[CH:]

    def halves(total, compute):
        for n in range(4):
            compute(total.sibling_piece(n))
            if n == 0 and total is one:
                pl.semaphore_wait(barrier, len(peers))
            total.send_sibling(n)
        for n in range(4):
            compute(total.own_piece(n))
            total.own_ready(n)
            if n == 2:
                total.pass_on()

    halves(one, left_piece)

    stores = []

    def merged_rows(i):
        rows = min(PIECE, TILE - i * PIECE)
        slot = i % 2
        if i >= 2:
            stores[i - 2].wait()
        for n in range(8):
            cols = min(PIECE, TILE - n * PIECE)
            r, k = pl.ds(i * PIECE, rows), pl.ds(n * PIECE, cols)
            stage[slot, pl.ds(0, rows), k] = mm_t(at[r, :], gt[k, :]) + e[r, k].astype(F32)
        made = pltpu.make_async_copy(
            stage.at[slot, pl.ds(0, rows)], merged_hbm.at[pl.ds(i * PIECE, rows)], stage_sem.at[slot]
        )
        made.start()
        stores.append(made)

    merged_rows(0)
    one.finish_first()
    one.second_start()
    merged_rows(1)
    merged_rows(2)
    one.second_pass_on()
    merged_rows(3)
    one.second_finish()
    one.third_start()
    merged_rows(4)
    merged_rows(5)
    one.third_pass_on()
    merged_rows(6)
    one.third_finish()
    merged_rows(7)
    one.wait_sibling()

    for i in range(NCH):
        t_hi, t_lo = split(y1[i].T)
        lt[:RANK, pl.ds(i * CH, CH)] = t_hi
        lt[RANK:, pl.ds(i * CH, CH)] = t_lo
    tokens(at)

    def right_piece(piece):
        rows = pl.ds(pl.multiple_of(piece * PIECE, PIECE), PIECE)
        v = mm_t(pt[...], gt[rows, :])
        v = v[:RANK] + v[RANK:]
        xs2[2 * piece] = v[:, :CH]
        xs2[2 * piece + 1] = v[:, CH:]

        @pl.when(piece < 7)
        def _():
            w = mm(lt[...], e[:, rows])
            w = w[:RANK] + w[RANK:]
            xs2[2 * piece] += w[:, :CH]
            xs2[2 * piece + 1] += w[:, CH:]

        @pl.when(piece == 7)
        def _():
            w = mm(lt[...], e[:, pl.ds(7 * PIECE, TILE - 7 * PIECE)])
            w = w[:RANK] + w[RANK:]
            xs2[14] += w[:, :CH]
            xs2[15, :, pl.ds(0, CH // 2)] += w[:, CH:]

    halves(two, right_piece)

    left = y1[...].reshape(PAD, RANK)
    row_i = lax.broadcasted_iota(jnp.int32, (RANK, RANK), 0)
    col_i = lax.broadcasted_iota(jnp.int32, (RANK, RANK), 1)
    gj[:, :RANK] = lax.dot_general(left, left, (((0,), (0,)), ((), ())), precision=PRECISE, preferred_element_type=F32)
    gj[:, RANK:] = jnp.where(row_i == col_i, 1.0, 0.0)

    def eliminate(first, count):
        def step(k, carry):
            row = gj[pl.ds(k, 1), :]
            whole = gj[...]
            pivot = jnp.sum(jnp.where(col_i[:1] == k, row[:, :RANK], 0.0), axis=1, keepdims=True)
            column = jnp.sum(jnp.where(col_i == k, whole[:, :RANK], 0.0), axis=1, keepdims=True)
            factor = jnp.where(row_i[:, :1] > k, column / pivot, 0.0)
            gj[...] = whole - factor * row
            return carry

        lax.fori_loop(first, first + count, step, 0)

    two.finish_first()
    two.second_start()
    eliminate(0, 32)
    two.second_pass_on()
    eliminate(32, 24)
    two.second_finish()
    two.third_start()
    eliminate(56, 32)
    two.third_pass_on()
    eliminate(88, 24)
    two.third_finish()
    eliminate(112, 16)
    diagonal = jnp.sum(jnp.where(row_i == col_i, gj[:, :RANK], 0.0), axis=1, keepdims=True)
    inverse = gj[:, RANK:] / jnp.sqrt(diagonal)

    for i in range(NCH):
        rows = min(CH, TILE - i * CH)
        o = lax.dot_general(y1[i], inverse, (((1,), (1,)), ((), ())), precision=PRECISE, preferred_element_type=F32)
        o_hi, o_lo = split(o[:rows])
        r = pl.ds(i * CH, rows)
        oo_ref[r, :RANK] = o_hi
        oo_ref[r, RANK : 2 * RANK] = o_hi
        oo_ref[r, 2 * RANK :] = o_lo
    two.wait_sibling()

    total = jnp.zeros((RANK, CH), F32)
    scaled = inverse / 32.0
    for i in range(NCH):
        rows = min(CH, TILE - i * CH)
        t = jnp.dot(scaled, y2[i], precision=PRECISE, preferred_element_type=F32)
        total = total + t * t
        qt[i] = t
        t_hi, t_lo = split(t[:, :rows])
        k = pl.ds(i * CH, rows)
        qq_ref[:RANK, k] = t_hi
        qq_ref[RANK : 2 * RANK, k] = t_lo
        qq_ref[2 * RANK :, k] = t_hi
    nb[y] = jnp.broadcast_to(jnp.sum(total), (8, RANK))
    gone = []
    for d in (1, 2, 3):
        made = pltpu.make_async_remote_copy(
            src_ref=nb.at[y],
            dst_ref=nb.at[y],
            send_sem=n_send.at[d - 1],
            recv_sem=n_recv.at[d - 1],
            device_id=(z, x, c, lax.rem(y + d, 4)),
            device_id_type=MESH,
        )
        made.start()
        gone.append(made)
    for i in range(NCH):
        rows = min(CH, TILE - i * CH)
        qn_ref[pl.ds(i * CH, rows), :] = qt[i].T[:rows]
    for made in stores[-2:]:
        made.wait()
    one.wait_sends()
    two.wait_sends()
    for made in gone:
        made.wait()
    norm_ref[...] = (nb[0] + nb[1]) + (nb[2] + nb[3])


def compress(at, gt, error, q):
    any_spec = pl.BlockSpec(memory_space=pl.ANY)
    vmem = pl.BlockSpec(memory_space=pltpu.VMEM)
    chunks = lambda n: pltpu.VMEM((n, CH, RANK), F32)
    sums = [chunks(NCH), pltpu.VMEM((4, 2, CH, RANK), F32), chunks(6), chunks(2), chunks(8), chunks(NCH)]
    return pl.pallas_call(
        body,
        out_shape=(
            jax.ShapeDtypeStruct((TILE, TILE), F32),
            jax.ShapeDtypeStruct((TILE, 3 * RANK), BF16),
            jax.ShapeDtypeStruct((3 * RANK, TILE), BF16),
            jax.ShapeDtypeStruct((TILE, RANK), F32),
            jax.ShapeDtypeStruct((8, RANK), F32),
        ),
        in_specs=[any_spec] * 4,
        out_specs=(any_spec, vmem, vmem, vmem, vmem),
        scratch_shapes=[
            pltpu.VMEM((PAD, TOK), BF16),
            pltpu.VMEM((PAD, TOK), BF16),
            pltpu.VMEM((PAD, TILE), BF16),
            pltpu.VMEM((TILE, RANK), F32),
            pltpu.VMEM((TILE, 2 * RANK), BF16),
            pltpu.VMEM((2 * RANK, TOK), BF16),
            pltpu.VMEM((2 * RANK, PAD), BF16),
            pltpu.VMEM((2, PIECE, TILE), F32),
            pltpu.VMEM((RANK, 2 * RANK), F32),
            pltpu.VMEM((4, 8, RANK), F32),
            chunks(NCH),
            *sums,
            *sums,
            pltpu.SemaphoreType.DMA((4,)),
            pltpu.SemaphoreType.DMA((2,)),
            pltpu.SemaphoreType.DMA((2 * N_MSG,)),
            pltpu.SemaphoreType.DMA((2 * N_MSG,)),
            pltpu.SemaphoreType.DMA((3,)),
            pltpu.SemaphoreType.DMA((3,)),
        ],
        compiler_params=pltpu.CompilerParams(
            collective_id=0, has_side_effects=True, vmem_limit_bytes=56 * 1024 * 1024
        ),
        name="compress",
    )(at, gt, error, q)


def residual(merged, oo, qq):
    def block(m_ref, o_ref, q_ref, out_ref):
        for n in range(8):
            k = pl.ds(n * PIECE, min(PIECE, TILE - n * PIECE))
            out_ref[:, k] = (m_ref[:, k] - mm(o_ref[...], q_ref[:, k])).astype(BF16)

    rows = TILE // 4
    return pl.pallas_call(
        block,
        grid=(4,),
        out_shape=jax.ShapeDtypeStruct((TILE, TILE), BF16),
        in_specs=[
            pl.BlockSpec((rows, TILE), lambda i: (i, 0)),
            pl.BlockSpec((rows, 3 * RANK), lambda i: (i, 0)),
            pl.BlockSpec((3 * RANK, TILE), lambda i: (0, 0)),
        ],
        out_specs=pl.BlockSpec((rows, TILE), lambda i: (i, 0)),
        name="residual",
    )(merged, oo, qq)


def per_device(acts, grads, error, momentum, q_start):
    at, gt = acts[:, 0, :].T, grads[:, 0, :].T
    merged, oo, qq, q_tile, norm = compress(at, gt, error[0, 0], q_start[0])
    error_next = residual(merged, oo, qq)
    rms_value = jnp.sqrt(norm[0, 0] / (D * D))
    owned_rows = momentum.shape[1]
    basis_owned = lax.dynamic_slice_in_dim(oo, lax.axis_index(DP) * owned_rows, owned_rows, 0)
    update = jnp.dot(basis_owned, qq, preferred_element_type=F32)
    momentum_next = 0.9 * momentum[0] + 0.1 * update / (rms_value + 1e-06)
    return (error_next[None, None], momentum_next[None], q_tile[None])


def solution(mesh):
    split_mesh = Mesh(mesh.devices.reshape(4, 4, 2, mesh.shape["mp"]), (*DP, "mp"))
    in_specs = (
        P(DP, "mp", None),
        P(DP, "mp", None),
        P(DP, "mp", None, None),
        P("mp", DP, None),
        P("mp", None, None),
    )
    out_specs = (P(DP, "mp", None, None), P("mp", DP, None), P("mp", None, None))
    return jax.shard_map(
        per_device, mesh=split_mesh, in_specs=in_specs, out_specs=out_specs, check_vma=False
    )
```

profile of v0, /device:TPU:0, one launch (start us, length us, event | category | flops | bytes accessed | tf_op | source)
XLA Modules:
  0.0 99.4 jit_solution(2561808161158286759)
XLA Ops:
  0.6 80.4 %compress.1 = (f32[1984,1984]{1,0:T(8,128)}, bf16[1984,384]{1,0:T(8,128)(2,1)}, bf16[384,1984]{1,0:T(8,128)(2,1)}, f32[1984,128]{1,0:T(8,128)}, f32[8,128]{1,0:T(8,128)}) custom-call(bf16[1984,768]{1,0:T(8,128)(2,1)} %bitcast.18, bf16[1984,768]{1,0:T(8,128)(2,1)} %bitcast.19, bf16[1984,1984]{1,0:T(8,128)(2,1)} %bitcast.17, f32[1984,128]{1,0:T(8,128)} %bitcast.21), custom_call_target="tpu_custom_call" | custom-call | tf_op jit(solution)/shard_map/compress/pallas_call | solution.py:403
  81.1 1.2 %slice.3 = f32[1,1]{1,0:T(1,128)} slice(f32[8,128]{1,0:T(8,128)} %get-tuple-element.11), slice={[0:1], [0:1]} | slice | bytes 8 | tf_op jit(solution)/shard_map/slice | solution.py:467
  83.0 0.0 copy-start
  83.0 0.0 copy-start.2
  83.0 12.8 %residual.1 = bf16[1984,1984]{1,0:T(8,128)(2,1)} custom-call(f32[1984,1984]{1,0:T(8,128)} %get-tuple-element.8.m_ref, bf16[1984,384]{1,0:T(8,128)(2,1)} %get-tuple-element.9.o_ref, bf16[384,1984]{1,0:T(8,128)(2,1)} %get-tuple-element.10.q_ref), custom_call_target="tpu_custom_call" | custom-call | tf_op jit(solution)/shard_map/residual/pallas_call | solution.py:449
  95.8 0.0 copy-done
  95.8 0.0 copy-done.2
  95.8 0.0 copy-start.1
  95.8 1.4 %fusion.2 = f32[1,62,1984]{2,1,0:T(8,128)S(1)} fusion(bf16[384,1984]{1,0:T(8,128)(2,1)S(1)} %copy-done, f32[1,62,1984]{2,0,1:T(1,128)S(1)} %copy-done.2, f32[]{:T(128)} %bitcast.8, bf16[1984,384]{1,0:T(8,128)(2,1)} %get-tuple-element.9.o_ref, s32[]{:T(128)S(6)} %select_n.3), kind=kOutput, calls=%fused_computation.3 | convolution fusion | flops 94962176 | bytes 2557444 | tf_op jit(solution)/shard_map/dot_general | solution.py:470
  97.1 1.3 %copy.9 = f32[1,62,1984]{2,0,1:T(1,128)} copy(f32[1,62,1984]{2,1,0:T(8,128)S(1)} %fusion.2) | data formatting | bytes 984064
  98.5 0.0 copy-done.1
  98.5 1.0 copy.14
Async XLA Ops:
  83.0 12.8 %copy-start = (bf16[384,1984]{1,0:T(8,128)(2,1)S(1)}, bf16[384,1984]{1,0:T(8,128)(2,1)}, u32[]{:S(2)}) copy-start(bf16[384,1984]{1,0:T(8,128)(2,1)} %get-tuple-element.10.q_ref) | copy-start | bytes 4571140
  83.0 12.8 %copy-start.2 = (f32[1,62,1984]{2,0,1:T(1,128)S(1)}, f32[1,62,1984]{2,0,1:T(1,128)}, u32[]{:S(2)}) copy-start(f32[1,62,1984]{2,0,1:T(1,128)} %param.8) | copy-start | bytes 1476100
  95.8 2.7 %copy-start.1 = (f32[1984,128]{1,0:T(8,128)S(1)}, f32[1984,128]{1,0:T(8,128)}, u32[]{:S(2)}) copy-start(f32[1984,128]{1,0:T(8,128)} %get-tuple-element.12) | copy-start | bytes 3047428
where the time goes:
time: 99.6 us; the launch traced here: 99.4 us
  Pallas kernels  93.2 us (94%)
  local copies, waits for them, and re-layouts  3.47 us (3%)
  between operations  1.38 us (1%)
  matrix products  1.36 us (1%)
    pallas_call x1, Pallas kernels, compress(): pl.pallas_call(body, out_shape=(jax.ShapeDtypeStruct((TILE, TILE), F32),...  80.4 us
    pallas_call x1, Pallas kernels, residual(): pl.pallas_call(block, grid=(4,), out_shape=jax.ShapeDtypeStruct((TILE, TI...  12.8 us
    unnamed x8, local copies, waits for them, and re-layouts  2.28 us

commit v1 on v0

--- a/solution.py
+++ b/solution.py
@@ -21,6 +21,7 @@
 PRECISE = lax.Precision.HIGHEST
 ORDER = (2, 1, 3, 0)
 N_MSG = 27
+OWNED = 62
 
 
 def mm(a, b):
@@ -137,12 +138,14 @@
         lf, rt = 2 * lax.rem(self.q + 3, 4), 2 * lax.rem(self.q + 1, 4)
         self.s_on = self.spread_on(10, self.slots, self.s_sent, lf, rt, self.along_second(1), self.along_second(3))
 
-    def second_finish(self):
+    def second_finish(self, change):
         for made in (*self.s_sent[2:], *self.s_on):
             made.wait_recv()
         own = 8 * self.c + 2 * self.p
         for s in range(2):
-            self.out[own + s] = (self.slots[s] + self.slots[2 + s]) + (self.slots[4 + s] + self.slots[6 + s])
+            self.out[own + s] = change(
+                (self.slots[s] + self.slots[2 + s]) + (self.slots[4 + s] + self.slots[6 + s])
+            )
 
     def third_start(self):
         own = 8 * self.c + 2 * self.p
@@ -179,33 +182,46 @@
 
 def body(
     at_hbm, gt_hbm, e_hbm, q_hbm,
-    merged_hbm, oo_ref, qq_ref, qn_ref, norm_ref,
-    at, gt, e, q, qs, pt, lt, stage, gj, nb, qt,
+    merged_ref, oo_ref, qq_ref, qn_ref, own_ref, norm_ref,
+    at, gt, e, ep, q, qs, pt, lt, gj, of, nb, ns,
     xs1, sib1, buf1, relay1, slots1, y1,
     xs2, sib2, buf2, relay2, slots2, y2,
-    in_sem, stage_sem, send, recv, n_send, n_recv,
+    in_sem, send, recv, n_send, n_recv,
 ):
     z, x, c, y = (lax.axis_index(a) for a in (*DP, "mp"))
     pos = (z, x, c, y)
+    half = PAD // 2
     loads = [
         pltpu.make_async_copy(q_hbm, q, in_sem.at[0]),
         pltpu.make_async_copy(gt_hbm, gt.at[pl.ds(0, TILE)], in_sem.at[1]),
         pltpu.make_async_copy(at_hbm, at.at[pl.ds(0, TILE)], in_sem.at[2]),
-        pltpu.make_async_copy(e_hbm, e.at[pl.ds(0, TILE)], in_sem.at[3]),
     ]
+    low = pltpu.make_async_copy(e_hbm.at[pl.ds(0, half)], e.at[pl.ds(0, half)], in_sem.at[3])
+    high = pltpu.make_async_copy(e_hbm.at[pl.ds(half, TILE - half)], e.at[pl.ds(half, TILE - half)], in_sem.at[4])
     for load in loads:
         load.start()
+
+    def by_core(first, second):
+        pl.when(c == 0)(first)
+        pl.when(c == 1)(second)
+
+    by_core(high.start, low.start)
+    by_core(low.start, high.start)
     one = Sum(pos, (xs1, sib1, buf1, relay1, slots1, y1), (send, recv), 0)
     two = Sum(pos, (xs2, sib2, buf2, relay2, slots2, y2), (send, recv), N_MSG)
 
+    def plane(d, f):
+        return (*one.along_first(d)[:3], lax.rem(y + f, 4))
+
+    steps = [(d, f) for d in range(4) for f in range(4) if d or f]
     barrier = pltpu.get_barrier_semaphore()
-    peers = [one.along_first(1), one.along_first(3), one.along_second(1), one.along_second(3), one.sibling()]
-    peers += [(z, x, c, lax.rem(y + d, 4)) for d in (1, 2, 3)]
+    peers = [one.along_second(1), one.along_second(3), one.sibling(), *(plane(d, f) for d, f in steps)]
     for peer in peers:
         pl.semaphore_signal(barrier, inc=1, device_id=peer, device_id_type=MESH)
 
-    for ref in (at, gt, e):
+    for ref in (at, gt, e, ep):
         ref[pl.ds(TILE, PAD - TILE), :] = jnp.zeros((PAD - TILE, ref.shape[1]), BF16)
+    ep[:, pl.ds(TILE, PAD - TILE)] = jnp.zeros((PAD, PAD - TILE), BF16)
 
     loads[0].wait()
     hi, lo = split(q[...])
@@ -229,45 +245,43 @@
 
     tokens(gt)
     loads[2].wait()
-    loads[3].wait()
-
-    def left_piece(piece):
-        rows = pl.ds(pl.multiple_of(piece * PIECE, PIECE), PIECE)
-        v = mm(e[rows, :], qs[...]) + mm_t(at[rows, :], pt[...])
-        v = v[:, :RANK] + v[:, RANK:]
-        xs1[2 * piece] = v[:CH]
-        xs1[2 * piece + 1] = v[CH:]
-
-    def halves(total, compute):
-        for n in range(4):
-            compute(total.sibling_piece(n))
+    by_core(high.wait, low.wait)
+
+    def place(piece):
+        return pl.ds(pl.multiple_of(piece * PIECE, PIECE), PIECE)
+
+    def left_pieces(*pieces):
+        done = [mm(e[place(i), :], qs[...]) + mm_t(at[place(i), :], pt[...]) for i in pieces]
+        for piece, v in zip(pieces, done):
+            v = v[:, :RANK] + v[:, RANK:]
+            xs1[2 * piece] = v[:CH]
+            xs1[2 * piece + 1] = v[CH:]
+
+    def halves(total, compute, between):
+        for n in (0, 2):
+            compute(total.sibling_piece(n), total.sibling_piece(n + 1))
             if n == 0 and total is one:
                 pl.semaphore_wait(barrier, len(peers))
             total.send_sibling(n)
-        for n in range(4):
-            compute(total.own_piece(n))
-            total.own_ready(n)
-            if n == 2:
-                total.pass_on()
-
-    halves(one, left_piece)
-
-    stores = []
+            total.send_sibling(n + 1)
+        between()
+        compute(total.own_piece(0), total.own_piece(1))
+        total.own_ready(0)
+        total.own_ready(1)
+        compute(total.own_piece(2), total.own_piece(3))
+        total.own_ready(2)
+        total.pass_on()
+        total.own_ready(3)
+
+    halves(one, left_pieces, lambda: by_core(low.wait, high.wait))
 
     def merged_rows(i):
-        rows = min(PIECE, TILE - i * PIECE)
-        slot = i % 2
-        if i >= 2:
-            stores[i - 2].wait()
+        r = pl.ds(i * PIECE, min(PIECE, TILE - i * PIECE))
         for n in range(8):
-            cols = min(PIECE, TILE - n * PIECE)
-            r, k = pl.ds(i * PIECE, rows), pl.ds(n * PIECE, cols)
-            stage[slot, pl.ds(0, rows), k] = mm_t(at[r, :], gt[k, :]) + e[r, k].astype(F32)
-        made = pltpu.make_async_copy(
-            stage.at[slot, pl.ds(0, rows)], merged_hbm.at[pl.ds(i * PIECE, rows)], stage_sem.at[slot]
-        )
-        made.start()
-        stores.append(made)
+            k = pl.ds(n * PIECE, min(PIECE, TILE - n * PIECE))
+            stored = e[r, k]
+            ep[r, k] = stored
+            merged_ref[r, k] = mm_t(at[r, :], gt[k, :]) + stored.astype(F32)
 
     merged_rows(0)
     one.finish_first()
@@ -276,14 +290,14 @@
     merged_rows(2)
     one.second_pass_on()
     merged_rows(3)
-    one.second_finish()
+    merged_rows(4)
+    one.second_finish(lambda v: v)
     one.third_start()
-    merged_rows(4)
     merged_rows(5)
+    merged_rows(6)
     one.third_pass_on()
-    merged_rows(6)
+    merged_rows(7)
     one.third_finish()
-    merged_rows(7)
     one.wait_sibling()
 
     for i in range(NCH):
@@ -292,28 +306,14 @@
         lt[RANK:, pl.ds(i * CH, CH)] = t_lo
     tokens(at)
 
-    def right_piece(piece):
-        rows = pl.ds(pl.multiple_of(piece * PIECE, PIECE), PIECE)
-        v = mm_t(pt[...], gt[rows, :])
-        v = v[:RANK] + v[RANK:]
-        xs2[2 * piece] = v[:, :CH]
-        xs2[2 * piece + 1] = v[:, CH:]
-
-        @pl.when(piece < 7)
-        def _():
-            w = mm(lt[...], e[:, rows])
-            w = w[:RANK] + w[RANK:]
-            xs2[2 * piece] += w[:, :CH]
-            xs2[2 * piece + 1] += w[:, CH:]
-
-        @pl.when(piece == 7)
-        def _():
-            w = mm(lt[...], e[:, pl.ds(7 * PIECE, TILE - 7 * PIECE)])
-            w = w[:RANK] + w[RANK:]
-            xs2[14] += w[:, :CH]
-            xs2[15, :, pl.ds(0, CH // 2)] += w[:, CH:]
-
-    halves(two, right_piece)
+    def right_pieces(*pieces):
+        done = [mm(lt[...], ep[:, place(i)]) + mm_t(pt[...], gt[place(i), :]) for i in pieces]
+        for piece, v in zip(pieces, done):
+            v = v[:RANK] + v[RANK:]
+            xs2[2 * piece] = v[:, :CH]
+            xs2[2 * piece + 1] = v[:, CH:]
+
+    halves(two, right_pieces, lambda: None)
 
     left = y1[...].reshape(PAD, RANK)
     row_i = lax.broadcasted_iota(jnp.int32, (RANK, RANK), 0)
@@ -333,66 +333,88 @@
 
         lax.fori_loop(first, first + count, step, 0)
 
+    eliminate(0, 28)
     two.finish_first()
     two.second_start()
-    eliminate(0, 32)
+    eliminate(28, 48)
     two.second_pass_on()
-    eliminate(32, 24)
-    two.second_finish()
-    two.third_start()
-    eliminate(56, 32)
-    two.third_pass_on()
-    eliminate(88, 24)
-    two.third_finish()
-    eliminate(112, 16)
+    eliminate(76, 52)
     diagonal = jnp.sum(jnp.where(row_i == col_i, gj[:, :RANK], 0.0), axis=1, keepdims=True)
     inverse = gj[:, RANK:] / jnp.sqrt(diagonal)
-
+    scaled = inverse / 32.0
+    squares = []
+
+    def to_q(v):
+        t = jnp.dot(scaled, v, precision=PRECISE, preferred_element_type=F32)
+        squares.append(t * t)
+        return t
+
+    two.second_finish(to_q)
+    two.third_start()
+
+    mine = 4 * one.p + y
+    nb[mine] = jnp.broadcast_to(jnp.sum(squares[0] + squares[1]), (8, RANK))
+    gone = []
+
+    def exchange(i, ref, to):
+        made = pltpu.make_async_remote_copy(
+            src_ref=ref,
+            dst_ref=ref,
+            send_sem=n_send.at[i],
+            recv_sem=n_recv.at[i],
+            device_id=to,
+            device_id_type=MESH,
+        )
+        made.start()
+        gone.append(made)
+
+    for i, (d, f) in enumerate(steps):
+        exchange(i, nb.at[mine], plane(d, f))
+
+    def ortho(first, count):
+        for i in range(first, first + count):
+            rows = min(CH, TILE - i * CH)
+            o = lax.dot_general(
+                y1[i], inverse, (((1,), (1,)), ((), ())), precision=PRECISE, preferred_element_type=F32
+            )
+            of[pl.ds(i * CH, CH), :] = o
+            o_hi, o_lo = split(o[:rows])
+            r = pl.ds(i * CH, rows)
+            oo_ref[r, :RANK] = o_hi
+            oo_ref[r, RANK : 2 * RANK] = o_hi
+            oo_ref[r, 2 * RANK :] = o_lo
+
+    ortho(0, 8)
+    two.third_pass_on()
+    ortho(8, 8)
+    for made in gone:
+        made.wait_recv()
+    norm = nb[0]
+    for i in range(1, 16):
+        norm = norm + nb[i]
+    ns[c] = norm
+    exchange(len(steps), ns.at[c], one.sibling())
+    two.third_finish()
+    o_hi, o_lo = split(of[pl.ds(((z * 4 + x) * 2 + c) * OWNED, 64), :])
+    own_ref[:, :RANK] = o_hi
+    own_ref[:, RANK : 2 * RANK] = o_hi
+    own_ref[:, 2 * RANK :] = o_lo
+    one.wait_sends()
+    gone[-1].wait_recv()
+    norm_ref[...] = ns[0] + ns[1]
+    two.wait_sibling()
     for i in range(NCH):
         rows = min(CH, TILE - i * CH)
-        o = lax.dot_general(y1[i], inverse, (((1,), (1,)), ((), ())), precision=PRECISE, preferred_element_type=F32)
-        o_hi, o_lo = split(o[:rows])
-        r = pl.ds(i * CH, rows)
-        oo_ref[r, :RANK] = o_hi
-        oo_ref[r, RANK : 2 * RANK] = o_hi
-        oo_ref[r, 2 * RANK :] = o_lo
-    two.wait_sibling()
-
-    total = jnp.zeros((RANK, CH), F32)
-    scaled = inverse / 32.0
-    for i in range(NCH):
-        rows = min(CH, TILE - i * CH)
-        t = jnp.dot(scaled, y2[i], precision=PRECISE, preferred_element_type=F32)
-        total = total + t * t
-        qt[i] = t
+        t = y2[i]
         t_hi, t_lo = split(t[:, :rows])
         k = pl.ds(i * CH, rows)
         qq_ref[:RANK, k] = t_hi
         qq_ref[RANK : 2 * RANK, k] = t_lo
         qq_ref[2 * RANK :, k] = t_hi
-    nb[y] = jnp.broadcast_to(jnp.sum(total), (8, RANK))
-    gone = []
-    for d in (1, 2, 3):
-        made = pltpu.make_async_remote_copy(
-            src_ref=nb.at[y],
-            dst_ref=nb.at[y],
-            send_sem=n_send.at[d - 1],
-            recv_sem=n_recv.at[d - 1],
-            device_id=(z, x, c, lax.rem(y + d, 4)),
-            device_id_type=MESH,
-        )
-        made.start()
-        gone.append(made)
-    for i in range(NCH):
-        rows = min(CH, TILE - i * CH)
-        qn_ref[pl.ds(i * CH, rows), :] = qt[i].T[:rows]
-    for made in stores[-2:]:
-        made.wait()
-    one.wait_sends()
+        qn_ref[k, :] = t.T[:rows]
     two.wait_sends()
     for made in gone:
-        made.wait()
-    norm_ref[...] = (nb[0] + nb[1]) + (nb[2] + nb[3])
+        made.wait_send()
 
 
 def compress(at, gt, error, q):
@@ -403,72 +425,87 @@
     return pl.pallas_call(
         body,
         out_shape=(
-            jax.ShapeDtypeStruct((TILE, TILE), F32),
-            jax.ShapeDtypeStruct((TILE, 3 * RANK), BF16),
-            jax.ShapeDtypeStruct((3 * RANK, TILE), BF16),
-            jax.ShapeDtypeStruct((TILE, RANK), F32),
-            jax.ShapeDtypeStruct((8, RANK), F32),
+            pltpu.VMEM((TILE, TILE), F32),
+            pltpu.VMEM((TILE, 3 * RANK), BF16),
+            pltpu.VMEM((3 * RANK, TILE), BF16),
+            pltpu.VMEM((TILE, RANK), F32),
+            pltpu.VMEM((64, 3 * RANK), BF16),
+            pltpu.VMEM((8, RANK), F32),
         ),
         in_specs=[any_spec] * 4,
-        out_specs=(any_spec, vmem, vmem, vmem, vmem),
+        out_specs=(vmem,) * 6,
         scratch_shapes=[
             pltpu.VMEM((PAD, TOK), BF16),
             pltpu.VMEM((PAD, TOK), BF16),
             pltpu.VMEM((PAD, TILE), BF16),
+            pltpu.VMEM((PAD, PAD), BF16),
             pltpu.VMEM((TILE, RANK), F32),
             pltpu.VMEM((TILE, 2 * RANK), BF16),
             pltpu.VMEM((2 * RANK, TOK), BF16),
             pltpu.VMEM((2 * RANK, PAD), BF16),
-            pltpu.VMEM((2, PIECE, TILE), F32),
             pltpu.VMEM((RANK, 2 * RANK), F32),
-            pltpu.VMEM((4, 8, RANK), F32),
-            chunks(NCH),
+            pltpu.VMEM((PAD, RANK), F32),
+            pltpu.VMEM((16, 8, RANK), F32),
+            pltpu.VMEM((2, 8, RANK), F32),
             *sums,
             *sums,
-            pltpu.SemaphoreType.DMA((4,)),
-            pltpu.SemaphoreType.DMA((2,)),
+            pltpu.SemaphoreType.DMA((5,)),
             pltpu.SemaphoreType.DMA((2 * N_MSG,)),
             pltpu.SemaphoreType.DMA((2 * N_MSG,)),
-            pltpu.SemaphoreType.DMA((3,)),
-            pltpu.SemaphoreType.DMA((3,)),
+            pltpu.SemaphoreType.DMA((16,)),
+            pltpu.SemaphoreType.DMA((16,)),
         ],
         compiler_params=pltpu.CompilerParams(
-            collective_id=0, has_side_effects=True, vmem_limit_bytes=56 * 1024 * 1024
+            collective_id=0, has_side_effects=True, vmem_limit_bytes=42 * 1024 * 1024
         ),
         name="compress",
     )(at, gt, error, q)
 
 
-def residual(merged, oo, qq):
-    def block(m_ref, o_ref, q_ref, out_ref):
-        for n in range(8):
-            k = pl.ds(n * PIECE, min(PIECE, TILE - n * PIECE))
-            out_ref[:, k] = (m_ref[:, k] - mm(o_ref[...], q_ref[:, k])).astype(BF16)
-
+def finish(merged, oo, qq, qn, own, norm, momentum):
     rows = TILE // 4
+
+    def block(m_ref, o_ref, q_ref, n_ref, own_ref, norm_ref, mom_ref, out_ref, next_ref, qn_ref):
+        i = pl.program_id(0)
+        at = pl.ds(pl.multiple_of(i * rows, 16), rows)
+        columns = [pl.ds(n * PIECE, min(PIECE, TILE - n * PIECE)) for n in range(8)]
+        for k in columns:
+            out_ref[:, k] = (m_ref[at, k] - mm(o_ref[at, :], q_ref[:, k])).astype(BF16)
+        qn_ref[...] = n_ref[at, :]
+
+        @pl.when(i == 0)
+        def _():
+            rms = jnp.sqrt(norm_ref[:1, :1] / (D * D))
+            scale = 0.1 / (rms + 1e-6)
+            for k in columns:
+                next_ref[:, k] = 0.9 * mom_ref[:, k] + scale * mm(own_ref[...], q_ref[:, k])[:OWNED]
+
+    vmem = pl.BlockSpec(memory_space=pltpu.VMEM)
+    held = [pltpu.with_memory_space_constraint(v, pltpu.VMEM) for v in (merged, oo, qq, qn, own, norm)]
+    whole = pl.BlockSpec((OWNED, TILE), lambda i: (0, 0))
     return pl.pallas_call(
         block,
         grid=(4,),
-        out_shape=jax.ShapeDtypeStruct((TILE, TILE), BF16),
-        in_specs=[
+        out_shape=(
+            jax.ShapeDtypeStruct((TILE, TILE), BF16),
+            jax.ShapeDtypeStruct((OWNED, TILE), F32),
+            jax.ShapeDtypeStruct((TILE, RANK), F32),
+        ),
+        in_specs=[vmem] * 6 + [whole],
+        out_specs=(
             pl.BlockSpec((rows, TILE), lambda i: (i, 0)),
-            pl.BlockSpec((rows, 3 * RANK), lambda i: (i, 0)),
-            pl.BlockSpec((3 * RANK, TILE), lambda i: (0, 0)),
-        ],
-        out_specs=pl.BlockSpec((rows, TILE), lambda i: (i, 0)),
-        name="residual",
-    )(merged, oo, qq)
+            whole,
+            pl.BlockSpec((rows, RANK), lambda i: (i, 0)),
+        ),
+        compiler_params=pltpu.CompilerParams(vmem_limit_bytes=16 * 1024 * 1024),
+        name="finish",
+    )(*held, momentum)
 
 
 def per_device(acts, grads, error, momentum, q_start):
     at, gt = acts[:, 0, :].T, grads[:, 0, :].T
-    merged, oo, qq, q_tile, norm = compress(at, gt, error[0, 0], q_start[0])
-    error_next = residual(merged, oo, qq)
-    rms_value = jnp.sqrt(norm[0, 0] / (D * D))
-    owned_rows = momentum.shape[1]
-    basis_owned = lax.dynamic_slice_in_dim(oo, lax.axis_index(DP) * owned_rows, owned_rows, 0)
-    update = jnp.dot(basis_owned, qq, preferred_element_type=F32)
-    momentum_next = 0.9 * momentum[0] + 0.1 * update / (rms_value + 1e-06)
+    made = compress(at, gt, error[0, 0], q_start[0])
+    error_next, momentum_next, q_tile = finish(*made, momentum[0])
     return (error_next[None, None], momentum_next[None], q_tile[None])
 
 

time: 99.6 us -> 78.7 us (0.79)
  the two profiles are of different devices: /device:TPU:0 before, /device:TPU:1 now
where the time goes in v1:
time: 78.7 us; the launch traced here: 78.5 us
  Pallas kernels  75.4 us (96%)
  local copies, waits for them, and re-layouts  2.5 us (3%)
    pallas_call x1, Pallas kernels, compress(): pl.pallas_call(body, out_shape=(pltpu.VMEM((TILE, TILE), F32), pltpu.VMEM...  68.5 us
    pallas_call x1, Pallas kernels, finish(): pl.pallas_call(block, grid=(4,), out_shape=(jax.ShapeDtypeStruct((TILE, T...  6.86 us
    unnamed x2, local copies, waits for them, and re-layouts  2.5 us

profile of v1, /device:TPU:1, one launch (start us, length us, event | category | flops | bytes accessed | tf_op | source)
XLA Modules:
  0.0 78.5 jit_solution(5899034880098271146)
XLA Ops:
  0.6 1.2 %copy.11 = f32[1,62,1984]{2,1,0:T(8,128)S(1)} copy(f32[1,62,1984]{2,0,1:T(1,128)} %param.8) | data formatting | bytes 984064
  1.8 68.5 %compress.1 = (f32[1984,1984]{1,0:T(8,128)S(1)}, bf16[1984,384]{1,0:T(8,128)(2,1)S(1)}, bf16[384,1984]{1,0:T(8,128)(2,1)S(1)}, f32[1984,128]{1,0:T(8,128)S(1)}, ...) custom-call(bf16[1984,768]{1,0:T(8,128)(2,1)} %bitcast.17, bf16[1984,768]{1,0:T(8,128)(2,1)} %bitcast.18, ...), custom_call_target="tpu_custom_call" | custom-call | tf_op jit(solution)/shard_map/compress/pallas_call | solution.py:425
  70.4 6.9 %finish.1 = (bf16[1984,1984]{1,0:T(8,128)(2,1)}, f32[62,1984]{1,0:T(8,128)S(1)}, f32[1984,128]{1,0:T(8,128)}) custom-call(f32[1984,1984]{1,0:T(8,128)S(1)} %get-tuple-element.12.m_ref, bf16[1984,384]{1,0:T(8,128)(2,1)S(1)} %get-tuple-element.13.o_ref, bf16[384,1984]{1,0:T(8,128)(2,1)S(1)} %get-tuple-element.14.q_ref, ...), custom_call_target="tpu_custom_call" | custom-call | tf_op jit(solution)/shard_map/finish/pallas_call | solution.py:486
  77.2 1.3 %copy.8 = f32[1,62,1984]{2,0,1:T(1,128)} copy(f32[1,62,1984]{2,1,0:T(8,128)S(1)} %bitcast.15) | data formatting | bytes 984064

commit v2 on v1

v2 whole, which is shorter than its diff:
```python
import jax
import jax.numpy as jnp
from jax import lax
from jax.experimental import pallas as pl
from jax.experimental.pallas import tpu as pltpu
from jax.sharding import Mesh
from jax.sharding import PartitionSpec as P

D = 3968
DP = ("dp_0", "dp_1", "dp_2")
MESH = pl.DeviceIdType.MESH
TILE = 1984
PAD = 2048
RANK = 128
TOK = 768
CH = 128
NCH = 16
PIECE = 256
F32 = jnp.float32
BF16 = jnp.bfloat16
PRECISE = lax.Precision.HIGHEST
ORDER = (2, 1, 3, 0)
CHIPS = [(z, x) for z in ORDER for x in ORDER if z or x]
N_MSG = 35
OWNED = 62


def mm(a, b):
    return jnp.dot(a, b, preferred_element_type=F32)


def mm_t(a, b):
    return lax.dot_general(a, b, (((1,), (1,)), ((), ())), preferred_element_type=F32)


def split(v):
    hi = v.astype(BF16)
    return hi, (v - hi.astype(F32)).astype(BF16)


class Sum:
    def __init__(self, pos, bufs, sems, base):
        self.z, self.x, self.c, self.y = pos
        self.xs, self.sib, self.slots, self.out = bufs
        self.send, self.recv = sems
        self.base = base
        self.started = []
        self.r = 4 * self.z + self.x
        self.from_sibling, self.scattered, self.spread = {}, [], []

    def chip(self, dz, dx):
        return lax.rem(self.z + dz, 4), lax.rem(self.x + dx, 4)

    def sibling(self):
        return (self.z, self.x, 1 - self.c, self.y)

    def copy(self, i, src, dst, to):
        made = pltpu.make_async_remote_copy(
            src_ref=src,
            dst_ref=dst,
            send_sem=self.send.at[self.base + i],
            recv_sem=self.recv.at[self.base + i],
            device_id=to,
            device_id_type=MESH,
        )
        made.start()
        self.started.append(made)
        return made

    def sibling_piece(self, n):
        return 4 * (1 - self.c) + lax.rem(self.z + ORDER[n], 4)

    def own_piece(self, n):
        return 4 * self.c + lax.rem(self.z + ORDER[n], 4)

    def send_sibling(self, n):
        i = 4 * self.sibling_piece(n)
        self.from_sibling[n] = self.copy(n, self.xs.at[pl.ds(i, 4)], self.sib.at[n], self.sibling())

    def own_ready(self, n):
        i = pl.ds(4 * self.own_piece(n), 4)
        self.from_sibling[n].wait_recv()
        self.xs[i] = self.xs[i] + self.sib[n]
        for dx in ORDER:
            if not (ORDER[n] or dx):
                continue
            z, x = self.chip(ORDER[n], dx)
            made = self.copy(
                4 + len(self.scattered),
                self.xs.at[16 * self.c + 4 * z + x],
                self.slots.at[self.r],
                (z, x, self.c, self.y),
            )
            self.scattered.append(made)

    def finish_scatter(self, change):
        mine = 16 * self.c + self.r
        self.slots[self.r] = self.xs[mine]
        for made in self.scattered:
            made.wait_recv()
        total = self.slots[0]
        for i in range(1, 16):
            total = total + self.slots[i]
        self.out[mine] = change(total)
        part = self.out.at[mine]
        for n, (dz, dx) in enumerate(CHIPS):
            self.spread.append(self.copy(19 + n, part, part, (*self.chip(dz, dx), self.c, self.y)))

    def finish_spread(self):
        for made in self.spread:
            made.wait_recv()
        part = self.out.at[pl.ds(16 * self.c, 16)]
        self.to_sibling = self.copy(34, part, part, self.sibling())

    def wait_sibling(self):
        self.to_sibling.wait_recv()

    def wait_sends(self):
        for made in self.started:
            made.wait_send()


def body(
    at_hbm, gt_hbm, e_hbm, q_hbm,
    merged_ref, oo_ref, qq_ref, qn_ref, own_ref, norm_ref,
    at, gt, e, ep, q, qs, pt, lt, gj, of, nt, nb, ns,
    xs1, sib1, slots1, y1,
    xs2, sib2, slots2, y2,
    in_sem, send, recv, n_send, n_recv,
):
    z, x, c, y = (lax.axis_index(a) for a in (*DP, "mp"))
    pos = (z, x, c, y)
    half = PAD // 2
    loads = [
        pltpu.make_async_copy(q_hbm, q, in_sem.at[0]),
        pltpu.make_async_copy(gt_hbm, gt.at[pl.ds(0, TILE)], in_sem.at[1]),
        pltpu.make_async_copy(at_hbm, at.at[pl.ds(0, TILE)], in_sem.at[2]),
    ]
    low = pltpu.make_async_copy(e_hbm.at[pl.ds(0, half)], e.at[pl.ds(0, half)], in_sem.at[3])
    high = pltpu.make_async_copy(e_hbm.at[pl.ds(half, TILE - half)], e.at[pl.ds(half, TILE - half)], in_sem.at[4])
    for load in loads:
        load.start()

    def by_core(first, second):
        pl.when(c == 0)(first)
        pl.when(c == 1)(second)

    by_core(high.start, low.start)
    by_core(low.start, high.start)
    one = Sum(pos, (xs1, sib1, slots1, y1), (send, recv), 0)
    two = Sum(pos, (xs2, sib2, slots2, y2), (send, recv), N_MSG)

    tiles = [(z, x, c, lax.rem(y + d, 4)) for d in (1, 2, 3)]
    chips = [(*one.chip(dz, dx), c, y) for dz, dx in CHIPS]
    barrier = pltpu.get_barrier_semaphore()
    peers = [one.sibling(), *tiles, *chips]
    for peer in peers:
        pl.semaphore_signal(barrier, inc=1, device_id=peer, device_id_type=MESH)

    for ref in (at, gt, e, ep):
        ref[pl.ds(TILE, PAD - TILE), :] = jnp.zeros((PAD - TILE, ref.shape[1]), BF16)
    ep[:, pl.ds(TILE, PAD - TILE)] = jnp.zeros((PAD, PAD - TILE), BF16)

    loads[0].wait()
    hi, lo = split(q[...])
    qs[:, :RANK] = hi
    qs[:, RANK:] = lo
    for i in range(NCH):
        rows = min(CH, TILE - i * CH)
        t_hi, t_lo = split(q[pl.ds(i * CH, rows), :].T)
        lt[:RANK, pl.ds(i * CH, rows)] = t_hi
        lt[RANK:, pl.ds(i * CH, rows)] = t_lo
    lt[:, pl.ds(TILE, PAD - TILE)] = jnp.zeros((2 * RANK, PAD - TILE), BF16)
    loads[1].wait()

    def tokens(ref):
        for n in range(TOK // PIECE):
            cols = pl.ds(n * PIECE, PIECE)
            v = mm(lt[...], ref[:, cols])
            v_hi, v_lo = split(v[:RANK] + v[RANK:])
            pt[:RANK, cols] = v_hi
            pt[RANK:, cols] = v_lo

    tokens(gt)
    loads[2].wait()
    by_core(high.wait, low.wait)

    def place(piece):
        return pl.ds(pl.multiple_of(piece * PIECE, PIECE), PIECE)

    def left_pieces(*pieces):
        done = [mm(e[place(i), :], qs[...]) + mm_t(at[place(i), :], pt[...]) for i in pieces]
        for piece, v in zip(pieces, done):
            v = v[:, :RANK] + v[:, RANK:]
            xs1[pl.ds(4 * piece, 4)] = v.reshape(4, 64, RANK)

    def halves(total, compute, between):
        for n in (0, 2):
            compute(total.sibling_piece(n), total.sibling_piece(n + 1))
            if n == 0 and total is one:
                pl.semaphore_wait(barrier, len(peers))
            total.send_sibling(n)
            total.send_sibling(n + 1)
        between()
        compute(total.own_piece(0), total.own_piece(1))
        total.own_ready(0)
        total.own_ready(1)
        compute(total.own_piece(2), total.own_piece(3))
        total.own_ready(2)
        total.own_ready(3)

    halves(one, left_pieces, lambda: by_core(low.wait, high.wait))

    def merged_rows(i):
        r = pl.ds(i * PIECE, min(PIECE, TILE - i * PIECE))
        for n in range(8):
            k = pl.ds(n * PIECE, min(PIECE, TILE - n * PIECE))
            stored = e[r, k]
            ep[r, k] = stored
            merged_ref[r, k] = mm_t(at[r, :], gt[k, :]) + stored.astype(F32)

    for i in range(4):
        merged_rows(i)
    one.finish_scatter(lambda v: v)
    for i in range(4, 8):
        merged_rows(i)
    one.finish_spread()
    one.wait_sibling()

    for i in range(NCH):
        t_hi, t_lo = split(y1[pl.ds(2 * i, 2)].reshape(CH, RANK).T)
        lt[:RANK, pl.ds(i * CH, CH)] = t_hi
        lt[RANK:, pl.ds(i * CH, CH)] = t_lo
    tokens(at)

    def right_pieces(*pieces):
        done = [mm(lt[...], ep[:, place(i)]) + mm_t(pt[...], gt[place(i), :]) for i in pieces]
        for piece, v in zip(pieces, done):
            xs2[pl.ds(4 * piece, 4)] = (v[:RANK] + v[RANK:]).T.reshape(4, 64, RANK)

    halves(two, right_pieces, lambda: None)

    left = y1[...].reshape(PAD, RANK)
    row_i = lax.broadcasted_iota(jnp.int32, (RANK, RANK), 0)
    col_i = lax.broadcasted_iota(jnp.int32, (RANK, RANK), 1)
    gj[:, :RANK] = lax.dot_general(left, left, (((0,), (0,)), ((), ())), precision=PRECISE, preferred_element_type=F32)
    gj[:, RANK:] = jnp.where(row_i == col_i, 1.0, 0.0)

    def eliminate(first, count):
        def step(k, carry):
            row = gj[pl.ds(k, 1), :]
            whole = gj[...]
            pivot = jnp.sum(jnp.where(col_i[:1] == k, row[:, :RANK], 0.0), axis=1, keepdims=True)
            column = jnp.sum(jnp.where(col_i == k, whole[:, :RANK], 0.0), axis=1, keepdims=True)
            factor = jnp.where(row_i[:, :1] > k, column / pivot, 0.0)
            gj[...] = whole - factor * row
            return carry

        lax.fori_loop(first, first + count, step, 0)

    eliminate(0, RANK)
    diagonal = jnp.sum(jnp.where(row_i == col_i, gj[:, :RANK], 0.0), axis=1, keepdims=True)
    inverse = gj[:, RANK:] / jnp.sqrt(diagonal)
    scaled = inverse / 32.0
    squares = []

    def to_q(v):
        t = lax.dot_general(v, scaled, (((1,), (1,)), ((), ())), precision=PRECISE, preferred_element_type=F32)
        squares.append(t * t)
        return t

    two.finish_scatter(to_q)

    gone = []

    def exchange(i, ref, to):
        made = pltpu.make_async_remote_copy(
            src_ref=ref,
            dst_ref=ref,
            send_sem=n_send.at[i],
            recv_sem=n_recv.at[i],
            device_id=to,
            device_id_type=MESH,
        )
        made.start()
        gone.append(made)

    nt[y] = jnp.broadcast_to(jnp.sum(squares[0]), (8, RANK))
    for i, to in enumerate(tiles):
        exchange(i, nt.at[y], to)

    def ortho(first, count):
        for i in range(first, first + count):
            rows = min(CH, TILE - i * CH)
            o = lax.dot_general(
                y1[pl.ds(2 * i, 2)].reshape(CH, RANK), inverse, (((1,), (1,)), ((), ())), precision=PRECISE, preferred_element_type=F32
            )
            of[pl.ds(i * CH, CH), :] = o
            o_hi, o_lo = split(o[:rows])
            r = pl.ds(i * CH, rows)
            oo_ref[r, :RANK] = o_hi
            oo_ref[r, RANK : 2 * RANK] = o_hi
            oo_ref[r, 2 * RANK :] = o_lo

    ortho(0, NCH)
    for made in gone:
        made.wait_recv()
    nb[one.r] = (nt[0] + nt[1]) + (nt[2] + nt[3])
    for i, to in enumerate(chips):
        exchange(3 + i, nb.at[one.r], to)
    two.finish_spread()
    o_hi, o_lo = split(of[pl.ds(((z * 4 + x) * 2 + c) * OWNED, 64), :])
    own_ref[:, :RANK] = o_hi
    own_ref[:, RANK : 2 * RANK] = o_hi
    own_ref[:, 2 * RANK :] = o_lo
    one.wait_sends()
    for made in gone[3:]:
        made.wait_recv()
    norm = nb[0]
    for i in range(1, 16):
        norm = norm + nb[i]
    ns[c] = norm
    exchange(18, ns.at[c], one.sibling())
    two.wait_sibling()
    t = y2[...].reshape(PAD, RANK)[:TILE]
    t_hi, t_lo = split(t)
    qq_ref[:, :RANK] = t_hi
    qq_ref[:, RANK : 2 * RANK] = t_lo
    qq_ref[:, 2 * RANK :] = t_hi
    qn_ref[...] = t
    gone[-1].wait_recv()
    norm_ref[...] = ns[0] + ns[1]
    two.wait_sends()
    for made in gone:
        made.wait_send()


def compress(at, gt, error, q):
    any_spec = pl.BlockSpec(memory_space=pl.ANY)
    vmem = pl.BlockSpec(memory_space=pltpu.VMEM)
    parts = lambda n: pltpu.VMEM((n, 64, RANK), F32)
    sums = [parts(32), pltpu.VMEM((4, 4, 64, RANK), F32), parts(16), parts(32)]
    return pl.pallas_call(
        body,
        out_shape=(
            pltpu.VMEM((TILE, TILE), F32),
            pltpu.VMEM((TILE, 3 * RANK), BF16),
            pltpu.VMEM((TILE, 3 * RANK), BF16),
            pltpu.VMEM((TILE, RANK), F32),
            pltpu.VMEM((64, 3 * RANK), BF16),
            pltpu.VMEM((8, RANK), F32),
        ),
        in_specs=[any_spec] * 4,
        out_specs=(vmem,) * 6,
        scratch_shapes=[
            pltpu.VMEM((PAD, TOK), BF16),
            pltpu.VMEM((PAD, TOK), BF16),
            pltpu.VMEM((PAD, TILE), BF16),
            pltpu.VMEM((PAD, PAD), BF16),
            pltpu.VMEM((TILE, RANK), F32),
            pltpu.VMEM((TILE, 2 * RANK), BF16),
            pltpu.VMEM((2 * RANK, TOK), BF16),
            pltpu.VMEM((2 * RANK, PAD), BF16),
            pltpu.VMEM((RANK, 2 * RANK), F32),
            pltpu.VMEM((PAD, RANK), F32),
            pltpu.VMEM((4, 8, RANK), F32),
            pltpu.VMEM((16, 8, RANK), F32),
            pltpu.VMEM((2, 8, RANK), F32),
            *sums,
            *sums,
            pltpu.SemaphoreType.DMA((5,)),
            pltpu.SemaphoreType.DMA((2 * N_MSG,)),
            pltpu.SemaphoreType.DMA((2 * N_MSG,)),
            pltpu.SemaphoreType.DMA((19,)),
            pltpu.SemaphoreType.DMA((19,)),
        ],
        compiler_params=pltpu.CompilerParams(
            collective_id=0, has_side_effects=True, vmem_limit_bytes=42 * 1024 * 1024
        ),
        name="compress",
    )(at, gt, error, q)


def finish(merged, oo, qq, qn, own, norm, momentum):
    rows = TILE // 4

    def block(m_ref, o_ref, q_ref, n_ref, own_ref, norm_ref, mom_ref, out_ref, next_ref, qn_ref):
        i = pl.program_id(0)
        at = pl.ds(pl.multiple_of(i * rows, 16), rows)
        columns = [pl.ds(n * PIECE, min(PIECE, TILE - n * PIECE)) for n in range(8)]
        for k in columns:
            out_ref[:, k] = (m_ref[at, k] - mm_t(o_ref[at, :], q_ref[k, :])).astype(BF16)
        qn_ref[...] = n_ref[at, :]

        @pl.when(i == 0)
        def _():
            rms = jnp.sqrt(norm_ref[:1, :1] / (D * D))
            scale = 0.1 / (rms + 1e-6)
            for k in columns:
                next_ref[:, k] = 0.9 * mom_ref[:, k] + scale * mm_t(own_ref[...], q_ref[k, :])[:OWNED]

    vmem = pl.BlockSpec(memory_space=pltpu.VMEM)
    held = [pltpu.with_memory_space_constraint(v, pltpu.VMEM) for v in (merged, oo, qq, qn, own, norm)]
    whole = pl.BlockSpec((OWNED, TILE), lambda i: (0, 0))
    return pl.pallas_call(
        block,
        grid=(4,),
        out_shape=(
            jax.ShapeDtypeStruct((TILE, TILE), BF16),
            jax.ShapeDtypeStruct((OWNED, TILE), F32),
            jax.ShapeDtypeStruct((TILE, RANK), F32),
        ),
        in_specs=[vmem] * 6 + [whole],
        out_specs=(
            pl.BlockSpec((rows, TILE), lambda i: (i, 0)),
            whole,
            pl.BlockSpec((rows, RANK), lambda i: (i, 0)),
        ),
        compiler_params=pltpu.CompilerParams(vmem_limit_bytes=16 * 1024 * 1024),
        name="finish",
    )(*held, momentum)


def per_device(acts, grads, error, momentum, q_start):
    at, gt = acts[:, 0, :].T, grads[:, 0, :].T
    made = compress(at, gt, error[0, 0], q_start[0])
    error_next, momentum_next, q_tile = finish(*made, momentum[0])
    return (error_next[None, None], momentum_next[None], q_tile[None])


def solution(mesh):
    split_mesh = Mesh(mesh.devices.reshape(4, 4, 2, mesh.shape["mp"]), (*DP, "mp"))
    in_specs = (
        P(DP, "mp", None),
        P(DP, "mp", None),
        P(DP, "mp", None, None),
        P("mp", DP, None),
        P("mp", None, None),
    )
    out_specs = (P(DP, "mp", None, None), P("mp", DP, None), P("mp", None, None))
    return jax.shard_map(
        per_device, mesh=split_mesh, in_specs=in_specs, out_specs=out_specs, check_vma=False
    )
```

time: 78.7 us -> 73.5 us (0.934)
  Pallas kernels: 75.4 us -> 70.2 us
    pallas_call x1, Pallas kernels: 68.5 us -> 63 us  [compress(): pl.pallas_call(body, out_shape=(pltpu.VMEM((TILE, TILE), F32), pltpu.VMEM...]
where the time goes in v2:
time: 73.5 us; the launch traced here: 73.4 us
  Pallas kernels  70.2 us (96%)
  local copies, waits for them, and re-layouts  2.5 us (3%)
    pallas_call x1, Pallas kernels, compress(): pl.pallas_call(body, out_shape=(pltpu.VMEM((TILE, TILE), F32), pltpu.VMEM...  63 us
    pallas_call x1, Pallas kernels, finish(): pl.pallas_call(block, grid=(4,), out_shape=(jax.ShapeDtypeStruct((TILE, T...  7.21 us
    unnamed x2, local copies, waits for them, and re-layouts  2.5 us

profile of v2, /device:TPU:1, one launch (start us, length us, event | category | flops | bytes accessed | tf_op | source)
XLA Modules:
  0.0 73.4 jit_solution(2234036811440456504)
XLA Ops:
  0.6 1.2 %copy.11 = f32[1,62,1984]{2,1,0:T(8,128)S(1)} copy(f32[1,62,1984]{2,0,1:T(1,128)} %param.8) | data formatting | bytes 984064
  1.8 63.0 %compress.1 = (f32[1984,1984]{1,0:T(8,128)S(1)}, bf16[1984,384]{1,0:T(8,128)(2,1)S(1)}, bf16[1984,384]{1,0:T(8,128)(2,1)S(1)}, f32[1984,128]{1,0:T(8,128)S(1)}, ...) custom-call(bf16[1984,768]{1,0:T(8,128)(2,1)} %bitcast.17, bf16[1984,768]{1,0:T(8,128)(2,1)} %bitcast.18, ...), custom_call_target="tpu_custom_call" | custom-call | tf_op jit(solution)/shard_map/compress/pallas_call | solution.py:343
  64.8 7.2 %finish.1 = (bf16[1984,1984]{1,0:T(8,128)(2,1)}, f32[62,1984]{1,0:T(8,128)S(1)}, f32[1984,128]{1,0:T(8,128)}) custom-call(f32[1984,1984]{1,0:T(8,128)S(1)} %get-tuple-element.12.m_ref, bf16[1984,384]{1,0:T(8,128)(2,1)S(1)} %get-tuple-element.13.o_ref, bf16[1984,384]{1,0:T(8,128)(2,1)S(1)} %get-tuple-element.14.q_ref, ...), custom_call_target="tpu_custom_call" | custom-call | tf_op jit(solution)/shard_map/finish/pallas_call | solution.py:405
  72.1 1.3 %copy.8 = f32[1,62,1984]{2,0,1:T(1,128)} copy(f32[1,62,1984]{2,1,0:T(8,128)S(1)} %bitcast.15) | data formatting | bytes 984064

commit v3 on v2

--- a/solution.py
+++ b/solution.py
@@ -246,19 +246,37 @@
     gj[:, :RANK] = lax.dot_general(left, left, (((0,), (0,)), ((), ())), precision=PRECISE, preferred_element_type=F32)
     gj[:, RANK:] = jnp.where(row_i == col_i, 1.0, 0.0)
 
-    def eliminate(first, count):
-        def step(k, carry):
-            row = gj[pl.ds(k, 1), :]
-            whole = gj[...]
-            pivot = jnp.sum(jnp.where(col_i[:1] == k, row[:, :RANK], 0.0), axis=1, keepdims=True)
-            column = jnp.sum(jnp.where(col_i == k, whole[:, :RANK], 0.0), axis=1, keepdims=True)
-            factor = jnp.where(row_i[:, :1] > k, column / pivot, 0.0)
-            gj[...] = whole - factor * row
+    def eliminate(first, count, width):
+        live = pl.ds(first, RANK - first)
+        row_at = lax.broadcasted_iota(jnp.int32, (RANK - first, 1), 0) + first
+        lane = col_i[:1]
+
+        def pick(v, k):
+            return jnp.sum(jnp.where(lane == k, v[:, :RANK], 0.0), axis=1, keepdims=True)
+
+        def step(n, carry):
+            k = first + width * n
+            whole = gj[live, :]
+            rows = [gj[pl.ds(k + i, 1), :] for i in range(width)]
+            columns = [pick(whole, k + i) for i in range(width)]
+            block = [[pick(rows[i], k + j) for j in range(width)] for i in range(width)]
+            for i in range(width):
+                inverse = 1.0 / block[i][i]
+                factor = jnp.where(row_at > k + i, columns[i] * inverse, 0.0)
+                for j in range(i + 1, width):
+                    f = block[j][i] * inverse
+                    columns[j] = columns[j] - factor * block[i][j]
+                    rows[j] = rows[j] - f * rows[i]
+                    for m in range(i + 1, width):
+                        block[j][m] = block[j][m] - f * block[i][m]
+                whole = whole - factor * rows[i]
+            gj[live, :] = whole
             return carry
 
-        lax.fori_loop(first, first + count, step, 0)
-
-    eliminate(0, RANK)
+        lax.fori_loop(0, count // width, step, 0)
+
+    for first in range(0, RANK, RANK // 4):
+        eliminate(first, RANK // 4, 4)
     diagonal = jnp.sum(jnp.where(row_i == col_i, gj[:, :RANK], 0.0), axis=1, keepdims=True)
     inverse = gj[:, RANK:] / jnp.sqrt(diagonal)
     scaled = inverse / 32.0

time: 73.5 us -> 65.5 us (0.89)
  Pallas kernels: 70.2 us -> 62.2 us
    pallas_call x1, Pallas kernels: 63 us -> 55 us  [compress(): pl.pallas_call(body, out_shape=(pltpu.VMEM((TILE, TILE), F32), pltpu.VMEM...]
where the time goes in v3:
time: 65.5 us; the launch traced here: 65.3 us
  Pallas kernels  62.2 us (95%)
  local copies, waits for them, and re-layouts  2.5 us (4%)
    pallas_call x1, Pallas kernels, compress(): pl.pallas_call(body, out_shape=(pltpu.VMEM((TILE, TILE), F32), pltpu.VMEM...  55 us
    pallas_call x1, Pallas kernels, finish(): pl.pallas_call(block, grid=(4,), out_shape=(jax.ShapeDtypeStruct((TILE, T...  7.21 us
    unnamed x2, local copies, waits for them, and re-layouts  2.5 us

profile of v3, /device:TPU:1, one launch (start us, length us, event | category | flops | bytes accessed | tf_op | source)
XLA Modules:
  0.0 65.3 jit_solution(12371455973302566980)
XLA Ops:
  0.6 1.2 %copy.11 = f32[1,62,1984]{2,1,0:T(8,128)S(1)} copy(f32[1,62,1984]{2,0,1:T(1,128)} %param.8) | data formatting | bytes 984064
  1.8 55.0 %compress.1 = (f32[1984,1984]{1,0:T(8,128)S(1)}, bf16[1984,384]{1,0:T(8,128)(2,1)S(1)}, bf16[1984,384]{1,0:T(8,128)(2,1)S(1)}, f32[1984,128]{1,0:T(8,128)S(1)}, ...) custom-call(bf16[1984,768]{1,0:T(8,128)(2,1)} %bitcast.17, bf16[1984,768]{1,0:T(8,128)(2,1)} %bitcast.18, ...), custom_call_target="tpu_custom_call" | custom-call | tf_op jit(solution)/shard_map/compress/pallas_call | solution.py:361
  56.8 7.2 %finish.1 = (bf16[1984,1984]{1,0:T(8,128)(2,1)}, f32[62,1984]{1,0:T(8,128)S(1)}, f32[1984,128]{1,0:T(8,128)}) custom-call(f32[1984,1984]{1,0:T(8,128)S(1)} %get-tuple-element.12.m_ref, bf16[1984,384]{1,0:T(8,128)(2,1)S(1)} %get-tuple-element.13.o_ref, bf16[1984,384]{1,0:T(8,128)(2,1)S(1)} %get-tuple-element.14.q_ref, ...), custom_call_target="tpu_custom_call" | custom-call | tf_op jit(solution)/shard_map/finish/pallas_call | solution.py:423
  64.0 1.3 %copy.8 = f32[1,62,1984]{2,0,1:T(1,128)} copy(f32[1,62,1984]{2,1,0:T(8,128)S(1)} %bitcast.15) | data formatting | bytes 984064

commit v4 on v3

--- a/solution.py
+++ b/solution.py
@@ -121,9 +121,9 @@
 
 
 def body(
-    at_hbm, gt_hbm, e_hbm, q_hbm,
-    merged_ref, oo_ref, qq_ref, qn_ref, own_ref, norm_ref,
-    at, gt, e, ep, q, qs, pt, lt, gj, of, nt, nb, ns,
+    at_hbm, gt_hbm, e_hbm, q_hbm, mom_hbm,
+    merged_ref, oo_ref, qq_ref, qn_ref, own_ref, norm_ref, mom_ref,
+    at, gt, e, ep, q, qs, pt, lt, gj, of, nt, nb, ns, mom,
     xs1, sib1, slots1, y1,
     xs2, sib2, slots2, y2,
     in_sem, send, recv, n_send, n_recv,
@@ -147,6 +147,8 @@
 
     by_core(high.start, low.start)
     by_core(low.start, high.start)
+    last = pltpu.make_async_copy(mom_hbm, mom, in_sem.at[5])
+    last.start()
     one = Sum(pos, (xs1, sib1, slots1, y1), (send, recv), 0)
     two = Sum(pos, (xs2, sib2, slots2, y2), (send, recv), N_MSG)
 
@@ -222,6 +224,8 @@
     for i in range(4):
         merged_rows(i)
     one.finish_scatter(lambda v: v)
+    last.wait()
+    mom_ref[...] = mom[:, 0, :]
     for i in range(4, 8):
         merged_rows(i)
     one.finish_spread()
@@ -353,7 +357,7 @@
         made.wait_send()
 
 
-def compress(at, gt, error, q):
+def compress(at, gt, error, q, momentum):
     any_spec = pl.BlockSpec(memory_space=pl.ANY)
     vmem = pl.BlockSpec(memory_space=pltpu.VMEM)
     parts = lambda n: pltpu.VMEM((n, 64, RANK), F32)
@@ -367,9 +371,10 @@
             pltpu.VMEM((TILE, RANK), F32),
             pltpu.VMEM((64, 3 * RANK), BF16),
             pltpu.VMEM((8, RANK), F32),
+            pltpu.VMEM((OWNED, TILE), F32),
         ),
-        in_specs=[any_spec] * 4,
-        out_specs=(vmem,) * 6,
+        in_specs=[any_spec] * 5,
+        out_specs=(vmem,) * 7,
         scratch_shapes=[
             pltpu.VMEM((PAD, TOK), BF16),
             pltpu.VMEM((PAD, TOK), BF16),
@@ -384,9 +389,10 @@
             pltpu.VMEM((4, 8, RANK), F32),
             pltpu.VMEM((16, 8, RANK), F32),
             pltpu.VMEM((2, 8, RANK), F32),
+            pltpu.VMEM((OWNED, 1, TILE), F32),
             *sums,
             *sums,
-            pltpu.SemaphoreType.DMA((5,)),
+            pltpu.SemaphoreType.DMA((6,)),
             pltpu.SemaphoreType.DMA((2 * N_MSG,)),
             pltpu.SemaphoreType.DMA((2 * N_MSG,)),
             pltpu.SemaphoreType.DMA((19,)),
@@ -396,7 +402,7 @@
             collective_id=0, has_side_effects=True, vmem_limit_bytes=42 * 1024 * 1024
         ),
         name="compress",
-    )(at, gt, error, q)
+    )(at, gt, error, q, momentum)
 
 
 def finish(merged, oo, qq, qn, own, norm, momentum):
@@ -415,20 +421,20 @@
             rms = jnp.sqrt(norm_ref[:1, :1] / (D * D))
             scale = 0.1 / (rms + 1e-6)
             for k in columns:
-                next_ref[:, k] = 0.9 * mom_ref[:, k] + scale * mm_t(own_ref[...], q_ref[k, :])[:OWNED]
+                next_ref[:, 0, k] = 0.9 * mom_ref[:, k] + scale * mm_t(own_ref[...], q_ref[k, :])[:OWNED]
 
     vmem = pl.BlockSpec(memory_space=pltpu.VMEM)
-    held = [pltpu.with_memory_space_constraint(v, pltpu.VMEM) for v in (merged, oo, qq, qn, own, norm)]
-    whole = pl.BlockSpec((OWNED, TILE), lambda i: (0, 0))
+    held = [pltpu.with_memory_space_constraint(v, pltpu.VMEM) for v in (merged, oo, qq, qn, own, norm, momentum)]
+    whole = pl.BlockSpec((OWNED, 1, TILE), lambda i: (0, 0, 0))
     return pl.pallas_call(
         block,
         grid=(4,),
         out_shape=(
             jax.ShapeDtypeStruct((TILE, TILE), BF16),
-            jax.ShapeDtypeStruct((OWNED, TILE), F32),
+            jax.ShapeDtypeStruct((OWNED, 1, TILE), F32),
             jax.ShapeDtypeStruct((TILE, RANK), F32),
         ),
-        in_specs=[vmem] * 6 + [whole],
+        in_specs=[vmem] * 7,
         out_specs=(
             pl.BlockSpec((rows, TILE), lambda i: (i, 0)),
             whole,
@@ -436,14 +442,14 @@
         ),
         compiler_params=pltpu.CompilerParams(vmem_limit_bytes=16 * 1024 * 1024),
         name="finish",
-    )(*held, momentum)
+    )(*held)
 
 
 def per_device(acts, grads, error, momentum, q_start):
     at, gt = acts[:, 0, :].T, grads[:, 0, :].T
-    made = compress(at, gt, error[0, 0], q_start[0])
-    error_next, momentum_next, q_tile = finish(*made, momentum[0])
-    return (error_next[None, None], momentum_next[None], q_tile[None])
+    made = compress(at, gt, error[0, 0], q_start[0], jnp.swapaxes(momentum, 0, 1))
+    error_next, momentum_next, q_tile = finish(*made)
+    return (error_next[None, None], jnp.swapaxes(momentum_next, 0, 1), q_tile[None])
 
 
 def solution(mesh):

time: 65.5 us -> 63.2 us (0.965)
  local copies, waits for them, and re-layouts: 2.5 us -> 0 us
    unnamed x2 -> x0, local copies, waits for them, and re-layouts: 2.5 us -> none
where the time goes in v4:
time: 63.2 us; the launch traced here: 63.1 us
  Pallas kernels  62.4 us (99%)
  between operations  0.64 us (1%)
    pallas_call x1, Pallas kernels, compress(): pl.pallas_call(body, out_shape=(pltpu.VMEM((TILE, TILE), F32), pltpu.VMEM...  55 us
    pallas_call x1, Pallas kernels, finish(): pl.pallas_call(block, grid=(4,), out_shape=(jax.ShapeDtypeStruct((TILE, T...  7.42 us

profile of v4, /device:TPU:1, one launch (start us, length us, event | category | flops | bytes accessed | tf_op | source)
XLA Modules:
  0.0 63.1 jit_solution(3374861037490021220)
XLA Ops:
  0.6 55.0 %compress.1 = (f32[1984,1984]{1,0:T(8,128)S(1)}, bf16[1984,384]{1,0:T(8,128)(2,1)S(1)}, bf16[1984,384]{1,0:T(8,128)(2,1)S(1)}, f32[1984,128]{1,0:T(8,128)S(1)}, ...) custom-call(bf16[1984,768]{1,0:T(8,128)(2,1)} %bitcast.13, bf16[1984,768]{1,0:T(8,128)(2,1)} %bitcast.14, ...), custom_call_target="tpu_custom_call" | custom-call | tf_op jit(solution)/shard_map/compress/pallas_call | solution.py:365
  55.7 7.4 %finish.1 = (bf16[1984,1984]{1,0:T(8,128)(2,1)}, f32[62,1,1984]{2,1,0:T(1,128)}, f32[1984,128]{1,0:T(8,128)}) custom-call(f32[1984,1984]{1,0:T(8,128)S(1)} %get-tuple-element.13.m_ref, bf16[1984,384]{1,0:T(8,128)(2,1)S(1)} %get-tuple-element.14.o_ref, bf16[1984,384]{1,0:T(8,128)(2,1)S(1)} %get-tuple-element.15.q_ref, ...), custom_call_target="tpu_custom_call" | custom-call | tf_op jit(solution)/shard_map/finish/pallas_call | solution.py:429
